TPU v7x, 256 devices: a whole 4x4x8 slice. The times are simulated.
256 devices in a mesh: expert: 8 (over x_hi, y), dp: 32 (over x_lo, z, core).
Axes of the slice: x: 4 (x_hi: 2, x_lo: 2; x = x_hi * 2 + x_lo), y: 4, z: 8, core: 2. Of those that a mesh axis runs over, the one named last changes fastest.
Arguments:
- tokens: bfloat16 [2048, 4096], P(('expert', 'dp')), may hold values from -6 to 6
- routes: int32 [2048, 2], P(('expert', 'dp')), may hold values from 0 to 7, all different within a row; in each aligned block of 8 rows (0 to 7, 8 to 15, ...) at most 3 rows name the same one
- route_weights: float32 [2048, 2], P(('expert', 'dp')), may hold values from 0.2 to 1
- w_gate: bfloat16 [8, 4096, 14336], P('expert', None, 'dp'), may hold values from -0.09375 to 0.09375
- w_up: bfloat16 [8, 4096, 14336], P('expert', None, 'dp'), may hold values from -0.09375 to 0.09375
- w_down: bfloat16 [8, 14336, 4096], P('expert', 'dp'), may hold values from -0.046875 to 0.046875
Outputs:
- mixed: bfloat16 [2048, 4096], P(('expert', 'dp'))
Inputs may be any that keep to these rules, and one draw needn't show every extreme that they name: `routes`: within the rows of one device (aligned blocks of 8 rows) the two experts of a token differ and no expert is named more than 3 times; in every draw some block names some expert exactly 3 times. Every expert is named somewhere.
All inputs are finite; a program needn't handle non-finite values.
Results may differ from a plain program's by a relative error of at most 0.0057.
Values may be sent and summed in bfloat16 or wider, within the bound.
No kernel may reach another device: no remote copies, remote signals or barrier semaphores. Data moves between devices by JAX's collectives and lax.ppermute only.
A program may use at most 128 MiB of HBM per device.

v0:
```python
import jax
import jax.numpy as jnp
from jax import lax
from jax.sharding import PartitionSpec as P


def expert_projection(gate_local, up_local, down_local):

    def project(block_rows, first_row):
        gated = jnp.dot(block_rows, gate_local, preferred_element_type=jnp.float32)
        upward = jnp.dot(block_rows, up_local, preferred_element_type=jnp.float32)
        hidden = (jax.nn.silu(gated) * upward).astype(jnp.bfloat16)
        return jnp.dot(hidden, down_local, preferred_element_type=jnp.float32)

    return project


def local(tokens, routes, route_weights, w_gate, w_up, w_down):
    groups = lax.axis_size("expert")
    tok_count = tokens.shape[0]
    features = tokens.shape[1]
    capacity = 3 * tok_count // groups
    columns = groups * capacity
    listed = routes.reshape(2 * tok_count)
    chosen = (listed[:, None] == jnp.arange(groups, dtype=jnp.int32)[None, :]).astype(jnp.int32)
    before = jnp.cumsum(chosen, axis=0) - chosen
    column = listed * capacity + jnp.sum(before * chosen, axis=1)
    placing = (column[:, None] == jnp.arange(columns, dtype=jnp.int32)[None, :]).astype(
        jnp.bfloat16
    )
    placing = placing.reshape(tok_count, 2, columns)
    sending = jnp.sum(placing, axis=1)
    outgoing = jnp.einsum("tw,td->wd", sending, tokens, preferred_element_type=jnp.float32).astype(
        jnp.bfloat16
    )
    arrived = lax.all_to_all(
        outgoing.reshape(groups, capacity, features),
        "expert",
        split_axis=0,
        concat_axis=0,
        tiled=True,
    )
    arrived = arrived.reshape(columns, features)
    project = expert_projection(w_gate[0], w_up[0], w_down[0])
    partials = project(lax.all_gather(arrived, "dp", axis=0, tiled=True), jnp.int32(0))
    summed = lax.psum_scatter(partials, "dp", scatter_dimension=0, tiled=True)
    results = summed.astype(jnp.bfloat16).reshape(groups, capacity, features)
    returned = lax.all_to_all(results, "expert", split_axis=0, concat_axis=0, tiled=True).reshape(
        columns, features
    )
    picked = jnp.einsum("tkw,wd->tkd", placing, returned, preferred_element_type=jnp.float32)
    combined = jnp.sum(route_weights[:, :, None] * picked, axis=1)
    return combined.astype(jnp.bfloat16)


def solution(mesh):
    placed = (
        P(("expert", "dp"), None),
        P(("expert", "dp"), None),
        P(("expert", "dp"), None),
        P("expert", None, "dp"),
        P("expert", None, "dp"),
        P("expert", "dp", None),
    )
    return jax.shard_map(
        local, mesh=mesh, in_specs=placed, out_specs=P(("expert", "dp"), None), check_vma=False
    )
```

profile of v0, /device:TPU:8, one launch (start us, length us, event | category | flops | bytes accessed | tf_op | source)
XLA Modules:
  0.0 278.0 jit_solution(10584551748539052171)
XLA Ops:
  6.5 0.0 copy-start
  6.5 0.0 all-gather.2.cloned.1.call-start
  6.5 0.8 copy.13
  7.3 0.1 eq.51
  7.4 0.1 fusion.16
  7.5 0.2 select_reduce_fusion
  7.7 0.1 reduce_sum.33
  7.8 0.1 copy.15
  7.9 0.1 fusion.20
  8.0 0.0 copy-done
  8.0 0.3 convolution_convert_fusion
  8.2 0.1 reshape.54
  8.4 14.1 %all_to_all.10 = bf16[8,3,4096]{2,1,0:T(4,128)(2,1)S(1)} all-to-all(bf16[8,3,4096]{2,1,0:T(4,128)(2,1)S(1)} %reshape.54), channel_id=1, replica_groups=mesh['expert'=8,'dp'=32] {'expert'}, dimensions={0} | all-to-all | bytes 393216 | tf_op jit(solution)/shard_map/all_to_all | solution.py:36
  22.5 0.8 reshape.55
  23.3 0.0 all-gather.2.cloned.1.call-update
  23.3 0.0 reduce-scatter.2.cloned.1.call-start
  23.4 69.3 %all-gather.2.cloned.1.call-done = bf16[768,4096]{1,0:T(8,128)(2,1)} async-done(((bf16[24,4096]{1,0:T(8,128)(2,1)}), bf16[768,4096]{1,0:T(8,128)(2,1)}) %all-gather.2.cloned.1.call-update) | async-done | bytes 6291472 | tf_op jit(solution)/shard_map/all_gather | solution.py:45
  92.6 6.9 %fusion.4 = f32[768,448]{0,1:T(8,128)S(1)} fusion(bf16[768,4096]{1,0:T(8,128)(2,1)} %all-gather.2.cloned.1.call-done, bf16[1,4096,448]{1,2,0:T(8,128)(2,1)} %param.9), kind=kOutput, calls=%fused_computation.6 | convolution fusion | flops 2818572288 | bytes 11337728 | tf_op jit(solution)/shard_map/dot_general | solution.py:10
  99.5 17.9 %fusion = f32[768,4096]{1,0:T(8,128)} fusion(bf16[1,448,4096]{2,1,0:T(8,128)(2,1)} %param.11, bf16[768,4096]{1,0:T(8,128)(2,1)} %all-gather.2.cloned.1.call-done, bf16[1,4096,448]{1,2,0:T(8,128)(2,1)} %param.10, f32[768,448]{0,1:T(8,128)S(1)} %fusion.4), kind=kOutput, calls=%fused_computation.2 | convolution fusion | flops 5639208960 | bytes 27590656 | tf_op jit(solution)/shard_map/dot_general | solution.py:13
  117.4 0.0 copy-start.1
  117.4 0.0 reduce-scatter.2.cloned.1.call-update
  117.4 137.9 %reduce-scatter.2.cloned.1.call-done = f32[24,4096]{1,0:T(8,128)} async-done(((f32[768,4096]{1,0:T(8,128)}), f32[24,4096]{1,0:T(8,128)}) %reduce-scatter.2.cloned.1.call-update) | async-done | bytes 393232 | tf_op jit(solution)/shard_map/reduce_scatter | solution.py:46
  255.4 1.0 convert_element_type.25
  256.4 0.1 reshape.56
  256.5 13.6 %all_to_all.11 = bf16[8,3,4096]{2,1,0:T(4,128)(2,1)S(1)} all-to-all(bf16[8,3,4096]{2,1,0:T(4,128)(2,1)S(1)} %reshape.56), channel_id=1, replica_groups=mesh['expert'=8,'dp'=32] {'expert'}, dimensions={0} | all-to-all | bytes 393216 | tf_op jit(solution)/shard_map/all_to_all | solution.py:48
  270.2 0.2 reshape.58
  270.3 0.0 copy-done.1
  270.3 0.9 fusion.12
  (2 shorter events, 0.0 us)
Async XLA Ops:
  6.5 1.4 copy-start
  6.5 86.1 %all-gather.2.cloned.1.call-start = ((), (), s32[]{:S(2)}) async-start(), calls=%async_computation.3 | async-start | bytes 6488064 | tf_op jit(solution)/shard_map/all_gather | solution.py:45
  23.3 232.0 %reduce-scatter.2.cloned.1.call-start = ((), (), s32[]{:S(2)}) async-start(), calls=%async_computation.4 | async-start | bytes 12976128 | tf_op jit(solution)/shard_map/reduce_scatter | solution.py:46
  117.4 152.9 %copy-start.1 = (f32[8,2]{0,1:T(2,128)S(1)}, f32[8,2]{0,1:T(2,128)}, u32[]{:S(2)}) copy-start(f32[8,2]{0,1:T(2,128)} %param.8) | copy-start | bytes 196
Sparse Core Ops, SparseCore 0:
  23.4 69.1 all-gather.1
  117.6 137.7 reduce-scatter.1
where the time goes:
time: 278 us
  waiting for transfers between devices  207 us (74%)
  blocking collectives  27.7 us (10%)
  matrix products  25.9 us (9%)
  between operations  13.5 us (5%)
    reduce_scatter x1, waiting for transfers between devices, local(): summed = lax.psum_scatter(partials, 'dp', scatter_dimension=0, tiled=True)  138 us
    all_gather x1, waiting for transfers between devices, local(): lax.all_gather(arrived, 'dp', axis=0, tiled=True)  69.3 us
    dot_general x1, matrix products, project(): return jnp.dot(hidden, down_local, preferred_element_type=jnp.float32)  17.9 us
    all_to_all x1, blocking collectives, local(): lax.all_to_all(outgoing.reshape(groups, capacity, features), 'expert', sp...  14.1 us
    all_to_all x1, blocking collectives, local(): lax.all_to_all(results, 'expert', split_axis=0, concat_axis=0, tiled=True)  13.6 us
    dot_general x1, matrix products, project(): gated = jnp.dot(block_rows, gate_local, preferred_element_type=jnp.float32)  6.9 us
  transfers between devices with their start and end apart: 2, of which 2 were waited for; matrix products, arithmetic and copies ran while one was open for 0% of the time, Pallas kernels for 0%

commit v1 on v0

v1 whole, which is shorter than its diff:
```python
import jax
import jax.numpy as jnp
from jax import lax
from jax.sharding import Mesh
from jax.sharding import PartitionSpec as P
from jax.experimental import pallas as pl
from jax.experimental.pallas import tpu as pltpu

EXPERT = ("xh", "y")
LINE = ("xl", "z")
ALL = ("xh", "y", "xl", "z", "c")
PIECES = 3
CUTS = 4
SWAP = [(0, 1), (1, 0)]


def expert_kernel(
    own_ref, other_ref, gate_in, up_in, down_in, keep_ref, give_ref, gate, up, down, sems
):
    count, features = own_ref.shape
    depth = features // CUTS
    arriving = []
    for cut in range(CUTS):
        span = pl.ds(cut * depth, depth)
        arriving.append(
            (
                pltpu.make_async_copy(gate_in.at[:, span], gate.at[:, span], sems.at[cut]),
                pltpu.make_async_copy(up_in.at[:, span], up.at[:, span], sems.at[CUTS + cut]),
            )
        )
    last = pltpu.make_async_copy(down_in, down, sems.at[2 * CUTS])
    for pair in arriving:
        for copy in pair:
            copy.start()
    last.start()
    gated = jnp.zeros((2 * count, gate.shape[0]), jnp.float32)
    upward = jnp.zeros((2 * count, gate.shape[0]), jnp.float32)
    across = (((1,), (1,)), ((), ()))
    for cut in range(CUTS):
        span = pl.ds(cut * depth, depth)
        block = jnp.concatenate([own_ref[:, span], other_ref[:, span]], axis=0)
        for copy in arriving[cut]:
            copy.wait()
        gated += lax.dot_general(block, gate[:, span], across, preferred_element_type=jnp.float32)
        upward += lax.dot_general(block, up[:, span], across, preferred_element_type=jnp.float32)
    hidden = (gated / (1.0 + jnp.exp(-gated)) * upward).astype(jnp.bfloat16)
    last.wait()
    half = count // 2
    unit = count // 16
    for cut in range(CUTS):
        span = pl.ds(cut * depth, depth)
        part = jnp.dot(hidden, down[:, span], preferred_element_type=jnp.float32)
        for block in range(16):
            source = (block % 2) * half + (block // 2) * unit
            target = pl.ds(block * unit, unit)
            keep_ref[target, span] = part[source : source + unit]
            give_ref[target, span] = part[count + source : count + source + unit].astype(
                jnp.bfloat16
            )


def project(own, other, gate, up, down):
    count, features = own.shape
    units = gate.shape[0]
    whole = pl.BlockSpec(memory_space=pltpu.VMEM)
    outside = pl.BlockSpec(memory_space=pl.ANY)
    return pl.pallas_call(
        expert_kernel,
        out_shape=(
            jax.ShapeDtypeStruct((count, features), jnp.float32),
            jax.ShapeDtypeStruct((count, features), jnp.bfloat16),
        ),
        in_specs=[whole, whole, outside, outside, outside],
        out_specs=(whole, whole),
        scratch_shapes=[
            pltpu.VMEM((units, features), jnp.bfloat16),
            pltpu.VMEM((units, features), jnp.bfloat16),
            pltpu.VMEM((units, features), jnp.bfloat16),
            pltpu.SemaphoreType.DMA((2 * CUTS + 1,)),
        ],
        cost_estimate=pl.CostEstimate(
            flops=12 * count * features * units,
            bytes_accessed=6 * units * features + 10 * count * features,
            transcendentals=2 * count * units,
        ),
        compiler_params=pltpu.CompilerParams(vmem_limit_bytes=40 * 1024 * 1024),
        name="expert",
    )(own, other, gate, up, down)


def local(tokens, routes, route_weights, w_gate, w_up, w_down):
    groups = lax.axis_size("xh") * lax.axis_size("y")
    tok_count = tokens.shape[0]
    features = tokens.shape[1]
    capacity = 3 * tok_count // groups
    columns = groups * capacity
    listed = routes.reshape(2 * tok_count)
    chosen = (listed[:, None] == jnp.arange(groups, dtype=jnp.int32)[None, :]).astype(jnp.int32)
    before = jnp.cumsum(chosen, axis=0) - chosen
    column = listed * capacity + jnp.sum(before * chosen, axis=1)
    placing = (column[:, None] == jnp.arange(columns, dtype=jnp.int32)[None, :]).astype(
        jnp.bfloat16
    )
    placing = placing.reshape(tok_count, 2, columns)
    sending = jnp.sum(placing, axis=1)
    outgoing = jnp.einsum("tw,td->wd", sending, tokens, preferred_element_type=jnp.float32).astype(
        jnp.bfloat16
    )
    arrived = lax.all_to_all(
        outgoing.reshape(groups, capacity, features), EXPERT, split_axis=0, concat_axis=0, tiled=True
    )
    arrived = arrived.reshape(columns, features)
    step = columns // PIECES
    lined = [
        lax.all_gather(arrived[i * step : (i + 1) * step], LINE, axis=0, tiled=True)
        for i in range(PIECES)
    ]
    side = lax.axis_index("xl")
    gate = jnp.swapaxes(w_gate[0], 0, 1)
    up = jnp.swapaxes(w_up[0], 0, 1)
    finished = []
    give = None
    for own in lined:
        if give is not None:
            own, give = lax.optimization_barrier((own, give))
            pending.append((keep, lax.ppermute(give, "c", SWAP)))
        else:
            pending = []
        other = lax.ppermute(own, "c", SWAP)
        keep, give = project(own, other, gate, up, w_down[0])
    pending.append((keep, lax.ppermute(give, "c", SWAP)))
    for keep, swapped in pending:
        paired = (keep + swapped.astype(jnp.float32)).astype(jnp.bfloat16)
        along = lax.psum_scatter(paired, "z", scatter_dimension=0, tiled=True)
        mine = lax.dynamic_slice_in_dim(along, side * step, step)
        theirs = lax.dynamic_slice_in_dim(along, (1 - side) * step, step)
        crossed = lax.ppermute(theirs, "xl", SWAP)
        finished.append(
            (mine.astype(jnp.float32) + crossed.astype(jnp.float32)).astype(jnp.bfloat16)
        )
    results = jnp.concatenate(finished).reshape(groups, capacity, features)
    returned = lax.all_to_all(results, EXPERT, split_axis=0, concat_axis=0, tiled=True).reshape(
        columns, features
    )
    picked = jnp.einsum("tkw,wd->tkd", placing, returned, preferred_element_type=jnp.float32)
    combined = jnp.sum(route_weights[:, :, None] * picked, axis=1)
    return combined.astype(jnp.bfloat16)


def solution(mesh):
    fine = Mesh(mesh.devices.reshape(2, 4, 2, 8, 2), ALL)
    placed = (
        P(ALL, None),
        P(ALL, None),
        P(ALL, None),
        P(EXPERT, None, ("xl", "z", "c")),
        P(EXPERT, None, ("xl", "z", "c")),
        P(EXPERT, ("xl", "z", "c"), None),
    )
    return jax.shard_map(
        local, mesh=fine, in_specs=placed, out_specs=P(ALL, None), check_vma=False
    )
```

time: 278 us -> 377 us (1.36)
  waiting for transfers between devices: 207 us -> 283 us
  matrix products: 25.9 us -> 1.12 us
  Pallas kernels: 0 us -> 17.5 us
  local copies, waits for them, and re-layouts: 2.3 us -> 19.3 us
  other arithmetic: 1.4 us -> 7.93 us
  starting transfers between devices: 0.04 us -> 5.83 us
    all_gather x1 -> x3, waiting for transfers between devices: 69.3 us -> 175 us  [local(): lax.all_gather(arrived[i * step:(i + 1) * step], LINE, axis=0, tiled=True)]
    reduce_scatter x1 -> x3, waiting for transfers between devices: 138 us -> 91.9 us  [local(): along = lax.psum_scatter(paired, 'z', scatter_dimension=0, tiled=True)]
    dot_general x2 -> x0, matrix products: 24.8 us -> none  [the longest x1 17.9 us: project(): return jnp.dot(hidden, down_local, preferred_element_type=jnp.float32)]
    pallas_call x0 -> x3, Pallas kernels: none -> 17.5 us  [project(): pl.pallas_call(expert_kernel, out_shape=(jax.ShapeDtypeStruct((count, fea...]
    ppermute x0 -> x9, waiting for transfers between devices: none -> 14.9 us  [the longest x3 7.01 us: local(): pending.append((keep, lax.ppermute(give, 'c', SWAP)))]
    unnamed x5 -> x25, local copies, waits for them, and re-layouts: 0.79 us -> 15.2 us
    convert_element_type x1 -> x6, other arithmetic: 1.02 us -> 7.53 us  [the longest x3 4.95 us: local(): paired = (keep + swapped.astype(jnp.float32)).astype(jnp.bfloat16)]
    ppermute x0 -> x9, starting transfers between devices: none -> 5.45 us  [the longest x3 4.12 us: local(): crossed = lax.ppermute(theirs, 'xl', SWAP)]
  transfers between devices with their start and end apart: 2 -> 15, of which waited for: 2 -> 13; matrix products, arithmetic and copies ran while one was open for 0% -> 2% of each run, Pallas kernels for 0% -> 5%
where the time goes in v1:
time: 377 us; the launch traced here: 376 us
  waiting for transfers between devices  283 us (75%)
  blocking collectives  28 us (7%)
  local copies, waits for them, and re-layouts  19.3 us (5%)
  Pallas kernels  17.5 us (5%)
  between operations  13.6 us (4%)
  other arithmetic  7.93 us (2%)
  starting transfers between devices  5.83 us (2%)
    all_gather x3, waiting for transfers between devices, local(): lax.all_gather(arrived[i * step:(i + 1) * step], LINE, axis=0, tiled=True)  175 us
    reduce_scatter x3, waiting for transfers between devices, local(): along = lax.psum_scatter(paired, 'z', scatter_dimension=0, tiled=True)  91.9 us
    pallas_call x3, Pallas kernels, project(): pl.pallas_call(expert_kernel, out_shape=(jax.ShapeDtypeStruct((count, fea...  17.5 us
    unnamed x25, local copies, waits for them, and re-layouts  15.2 us
    all_to_all x1, blocking collectives, local(): lax.all_to_all(outgoing.reshape(groups, capacity, features), EXPERT, spli...  14.1 us
    all_to_all x1, blocking collectives, local(): lax.all_to_all(results, EXPERT, split_axis=0, concat_axis=0, tiled=True)  13.9 us
  transfers between devices with their start and end apart: 15, of which 13 were waited for; matrix products, arithmetic and copies ran while one was open for 2% of the time, Pallas kernels for 5%

profile of v1, /device:TPU:8, one launch (start us, length us, event | category | flops | bytes accessed | tf_op | source)
XLA Modules:
  0.0 375.8 jit_solution(14253955874587425032)
XLA Ops:
  8.4 14.1 %all_to_all.10 = bf16[8,3,4096]{2,1,0:T(4,128)(2,1)S(1)} all-to-all(bf16[8,3,4096]{2,1,0:T(4,128)(2,1)S(1)} %reshape.54), channel_id=1, replica_groups=mesh['xh'=2,'y'=4,'xl'=2,'z'=8,'c'=2] {'xh','y'}, dimensions={0} | all-to-all | bytes 393216 | tf_op jit(solution)/shard_map/all_to_all | solution.py:109
  24.1 68.4 %all-gather.4.cloned.1.call-done.own_ref = bf16[128,4096]{1,0:T(8,128)(2,1)} async-done(((bf16[8,4096]{1,0:T(8,128)(2,1)}), bf16[128,4096]{1,0:T(8,128)(2,1)}) %all-gather.4.cloned.1.call-update) | async-done | bytes 1048592 | tf_op jit(solution)/shard_map/all_gather | solution.py:115
  92.6 2.9 collective-permute-done.other_ref
  95.4 2.0 copy-done.1
  97.5 2.0 copy-done.4
  99.5 1.2 copy-done.9
  100.7 5.0 %expert.3 = (f32[128,4096]{1,0:T(8,128)S(1)}, bf16[128,4096]{1,0:T(8,128)(2,1)S(1)}) custom-call(bf16[128,4096]{1,0:T(8,128)(2,1)S(1)} %copy-done.9, bf16[128,4096]{1,0:T(8,128)(2,1)S(1)} %collective-permute-done.other_ref, bf16[448,4096]{1,0:T(8,128)(2,1)S(1)} %bitcast.13, bf16[448,4096]{1,0:T(8,128)(2,1)S(1)} %bitcast.16, bf16[448,4096]{1,0:T(8,128)(2,1)} %bitcast.19), custom_call_target="tpu_custom_call" | custom-call | flops 2818572288 | bytes 16252928 | tf_op jit(solution)/shard_map/expert/pallas_call | solution.py:67
  105.8 55.1 %all-gather.6.cloned.1.call-done.own_ref = bf16[128,4096]{1,0:T(8,128)(2,1)} async-done(((bf16[8,4096]{1,0:T(8,128)(2,1)}), bf16[128,4096]{1,0:T(8,128)(2,1)}) %all-gather.6.cloned.1.call-update) | async-done | bytes 1048592 | tf_op jit(solution)/shard_map/all_gather | solution.py:115
  161.6 2.1 collective-permute-done.1
  163.7 2.5 add_convert_fusion.2
  166.3 2.0 copy-done.2
  168.4 2.0 copy-done.5
  170.4 6.2 %expert.4 = (f32[128,4096]{1,0:T(8,128)S(1)}, bf16[128,4096]{1,0:T(8,128)(2,1)S(1)}) custom-call(bf16[128,4096]{1,0:T(8,128)(2,1)S(1)} %copy-done.8, bf16[128,4096]{1,0:T(8,128)(2,1)} %collective-permute-done.3.other_ref, bf16[448,4096]{1,0:T(8,128)(2,1)S(1)} %bitcast.14, bf16[448,4096]{1,0:T(8,128)(2,1)S(1)} %bitcast.17, bf16[448,4096]{1,0:T(8,128)(2,1)} %bitcast.20), custom_call_target="tpu_custom_call" | custom-call | flops 2818572288 | bytes 16252928 | tf_op jit(solution)/shard_map/expert/pallas_call | solution.py:67
  176.7 1.0 copy-done.10
  177.6 51.4 %all-gather.8.cloned.1.call-done.own_ref = bf16[128,4096]{1,0:T(8,128)(2,1)} async-done(((bf16[8,4096]{1,0:T(8,128)(2,1)}), bf16[128,4096]{1,0:T(8,128)(2,1)}) %all-gather.8.cloned.1.call-update) | async-done | bytes 1048592 | tf_op jit(solution)/shard_map/all_gather | solution.py:115
  229.5 2.4 collective-permute-done.4
  231.9 1.3 add_convert_fusion.1
  233.5 2.0 copy-done.3
  235.6 2.0 copy-done.6
  237.6 6.2 %expert.5 = (f32[128,4096]{1,0:T(8,128)S(1)}, bf16[128,4096]{1,0:T(8,128)(2,1)S(1)}) custom-call(bf16[128,4096]{1,0:T(8,128)(2,1)S(1)} %copy-done.7, bf16[128,4096]{1,0:T(8,128)(2,1)} %collective-permute-done.6.other_ref, bf16[448,4096]{1,0:T(8,128)(2,1)S(1)} %bitcast.15, bf16[448,4096]{1,0:T(8,128)(2,1)S(1)} %bitcast.18, bf16[448,4096]{1,0:T(8,128)(2,1)} %bitcast.21), custom_call_target="tpu_custom_call" | custom-call | flops 2818572288 | bytes 16252928 | tf_op jit(solution)/shard_map/expert/pallas_call | solution.py:67
  244.1 2.5 collective-permute-done.7
  246.6 1.2 add_convert_fusion
  247.8 19.8 %reduce-scatter.4.cloned.1.call-done = bf16[16,4096]{1,0:T(8,128)(2,1)} async-done(((bf16[128,4096]{1,0:T(8,128)(2,1)}), bf16[16,4096]{1,0:T(8,128)(2,1)}) %reduce-scatter.4.cloned.1.call-update) | async-done | bytes 131088 | tf_op jit(solution)/shard_map/reduce_scatter | solution.py:134
  268.5 1.3 collective-permute-start.2
  269.9 2.9 collective-permute-done.2
  273.6 34.2 %reduce-scatter.6.cloned.1.call-done = bf16[16,4096]{1,0:T(8,128)(2,1)} async-done(((bf16[128,4096]{1,0:T(8,128)(2,1)}), bf16[16,4096]{1,0:T(8,128)(2,1)}) %reduce-scatter.6.cloned.1.call-update) | async-done | bytes 131088 | tf_op jit(solution)/shard_map/reduce_scatter | solution.py:134
  308.6 1.4 collective-permute-start.5
  310.0 37.9 %reduce-scatter.8.cloned.1.call-done = bf16[16,4096]{1,0:T(8,128)(2,1)} async-done(((bf16[128,4096]{1,0:T(8,128)(2,1)}), bf16[16,4096]{1,0:T(8,128)(2,1)}) %reduce-scatter.8.cloned.1.call-update) | async-done | bytes 131088 | tf_op jit(solution)/shard_map/reduce_scatter | solution.py:134
  348.7 1.4 collective-permute-start.8
  351.0 2.0 collective-permute-done.8
  353.0 0.9 add_convert_fusion.3
  354.0 13.9 %all_to_all.11 = bf16[8,3,4096]{2,1,0:T(4,128)(2,1)S(1)} all-to-all(bf16[8,3,4096]{2,1,0:T(4,128)(2,1)S(1)} %reshape.56), channel_id=1, replica_groups=mesh['xh'=2,'y'=4,'xl'=2,'z'=8,'c'=2] {'xh','y'}, dimensions={0} | all-to-all | bytes 393216 | tf_op jit(solution)/shard_map/all_to_all | solution.py:142
  (59 shorter events, 10.7 us)
Async XLA Ops:
  6.5 1.4 copy-start
  6.5 86.0 %all-gather.4.cloned.1.call-start = ((), (), s32[]{:S(2)}) async-start(), calls=%async_computation.5 | async-start | bytes 1114112 | tf_op jit(solution)/shard_map/all_gather | solution.py:115
  23.3 137.6 %all-gather.6.cloned.1.call-start = ((), (), s32[]{:S(2)}) async-start(), calls=%async_computation.6 | async-start | bytes 1114112 | tf_op jit(solution)/shard_map/all_gather | solution.py:115
  24.1 205.0 %all-gather.8.cloned.1.call-start = ((), (), s32[]{:S(2)}) async-start(), calls=%async_computation.8 | async-start | bytes 1114112 | tf_op jit(solution)/shard_map/all_gather | solution.py:115
  92.6 2.9 collective-permute-start
  95.4 2.0 copy-start.1
  97.5 2.0 copy-start.4
  99.5 1.2 copy-start.9
  160.9 2.8 collective-permute-start.1
  160.9 106.7 %reduce-scatter.4.cloned.1.call-start = ((), (), s32[]{:S(2)}) async-start(), calls=%async_computation.7 | async-start | bytes 1179648 | tf_op jit(solution)/shard_map/reduce_scatter | solution.py:134
  161.0 5.3 %collective-permute-start.3 = (bf16[128,4096]{1,0:T(8,128)(2,1)}, bf16[128,4096]{1,0:T(8,128)(2,1)}, u32[]{:S(2)}, u32[]{:S(2)}) collective-permute-start(bf16[128,4096]{1,0:T(8,128)(2,1)} %all-gather.6.cloned.1.call-done.own_ref), channel_id=1, source_target_pairs={{0,1},{1,0},{2,3},{3,2},{4,5},{5,4},{6,7},{7,6},{8,9},{9,8},{10,11... | collective-permute-start | bytes 3145736 | tf_op jit(solution)/shard_map/ppermute | solution.py:129
  163.7 2.6 copy-start.8
  166.2 141.6 %reduce-scatter.6.cloned.1.call-start = ((), (), s32[]{:S(2)}) async-start(), calls=%async_computation.9 | async-start | bytes 1179648 | tf_op jit(solution)/shard_map/reduce_scatter | solution.py:134
  166.3 2.0 copy-start.2
  168.4 2.0 copy-start.5
  176.6 1.0 copy-start.10
  229.0 2.9 collective-permute-start.4
  229.0 4.5 %collective-permute-start.6 = (bf16[128,4096]{1,0:T(8,128)(2,1)}, bf16[128,4096]{1,0:T(8,128)(2,1)}, u32[]{:S(2)}, u32[]{:S(2)}) collective-permute-start(bf16[128,4096]{1,0:T(8,128)(2,1)} %all-gather.8.cloned.1.call-done.own_ref), channel_id=1, source_target_pairs={{0,1},{1,0},{2,3},{3,2},{4,5},{5,4},{6,7},{7,6},{8,9},{9,8},{10,11... | collective-permute-start | bytes 3145736 | tf_op jit(solution)/shard_map/ppermute | solution.py:129
  231.9 1.6 copy-start.7
  233.2 114.7 %reduce-scatter.8.cloned.1.call-start = ((), (), s32[]{:S(2)}) async-start(), calls=%async_computation.10 | async-start | bytes 1179648 | tf_op jit(solution)/shard_map/reduce_scatter | solution.py:134
  233.5 2.0 copy-start.3
  235.6 2.0 copy-start.6
  243.9 2.7 collective-permute-start.7
  247.8 120.3 %copy-start.11 = (f32[8,2]{0,1:T(2,128)S(1)}, f32[8,2]{0,1:T(2,128)}, u32[]{:S(2)}) copy-start(f32[8,2]{0,1:T(2,128)} %param.8) | copy-start | bytes 196
  268.5 4.3 %collective-permute-start.2 = (bf16[8,4096]{1,0:T(8,128)(2,1)S(1)}, bf16[8,4096]{1,0:T(8,128)(2,1)S(1)}, u32[]{:S(2)}, u32[]{:S(2)}) collective-permute-start(bf16[8,4096]{1,0:T(8,128)(2,1)S(1)} %constant_dynamic-slice_fusion.1), channel_id=1, source_target_pairs={{0,16},{16,0},{1,17},{17,1},{2,18},{18,2},{3,19},{19,3},{4,20},{20... | collective-permute-start | bytes 196616 | tf_op jit(solution)/shard_map/ppermute | solution.py:137
  308.6 41.5 %collective-permute-start.5 = (bf16[8,4096]{1,0:T(8,128)(2,1)S(1)}, bf16[8,4096]{1,0:T(8,128)(2,1)S(1)}, u32[]{:S(2)}, u32[]{:S(2)}) collective-permute-start(bf16[8,4096]{1,0:T(8,128)(2,1)S(1)} %constant_dynamic-slice_fusion), channel_id=1, source_target_pairs={{0,16},{16,0},{1,17},{17,1},{2,18},{18,2},{3,19},{19,3},{4,20},{20... | collective-permute-start | bytes 196616 | tf_op jit(solution)/shard_map/ppermute | solution.py:137
  348.7 4.3 %collective-permute-start.8 = (bf16[8,4096]{1,0:T(8,128)(2,1)S(1)}, bf16[8,4096]{1,0:T(8,128)(2,1)S(1)}, u32[]{:S(2)}, u32[]{:S(2)}) collective-permute-start(bf16[8,4096]{1,0:T(8,128)(2,1)S(1)} %constant_dynamic-slice_fusion.2), channel_id=1, source_target_pairs={{0,16},{16,0},{1,17},{17,1},{2,18},{18,2},{3,19},{19,3},{4,20},{20... | collective-permute-start | bytes 196616 | tf_op jit(solution)/shard_map/ppermute | solution.py:137
Sparse Core Ops, SparseCore 0:
  23.4 69.0 all-gather.3
  94.4 66.4 all-gather.5
  162.7 66.3 all-gather.7
  231.4 36.1 reduce-scatter.3
  270.0 37.7 reduce-scatter.5
  310.2 37.6 reduce-scatter.7
